TPU v7x, 128 devices: a whole 4x4x4 slice. The times are simulated.
128 devices in a mesh: pop: 8 (over y_lo, x), col: 16 (over z, y_hi, core).
Axes of the slice: x: 4, y: 4 (y_hi: 2, y_lo: 2; y = y_hi * 2 + y_lo), z: 4, core: 2. Of those that a mesh axis runs over, the one named last changes fastest.
Arguments:
- acts: bfloat16 [128, 64, 3584], P('pop', None, 'col'), may hold values from -6 to 6
- weight: bfloat16 [3584, 18944], P('pop', 'col'), may hold values from -0.09375 to 0.09375
- input_noise_factor: bfloat16 [128, 4, 3584], P('pop'), may hold values from -1 to 1
- output_noise_factor: bfloat16 [128, 4, 18944], P('pop', None, 'col'), may hold values from -8 to 8
- ranks: int32 [128], P('pop'), may hold values from 0 to 127, each once
Outputs:
- member_out: bfloat16 [128, 64, 18944], P('pop', None, 'col')
- step_dir: float32 [3584, 18944], P('pop', 'col')
- new_weight: bfloat16 [3584, 18944], P('pop', 'col')
Inputs may be any that keep to these rules, and one draw needn't show every extreme that they name: `ranks`: every member has a different rank.
All inputs are finite; a program needn't handle non-finite values.
Results may differ from a plain program's by a relative error of at most 0.0034.
Values may be sent and summed in bfloat16 or wider, within the bound.
A program may use at most 192 MiB of HBM per device.

v0:
```python
import jax
import jax.numpy as jnp
from jax import lax
from jax.sharding import PartitionSpec as P

D = 3584
F = 18944


def body(acts, weight, input_noise_factor, output_noise_factor, ranks):
    whole = lax.all_gather(acts, "col", axis=2, tiled=True)
    members, tokens, width = whole.shape
    flat = whole.reshape(members * tokens, width)
    base = jnp.dot(
        flat, lax.all_gather(weight, "pop", axis=0, tiled=True), preferred_element_type=jnp.float32
    )
    lower_bound = jnp.einsum(
        "mtd,mrd->mtr", whole, input_noise_factor, preferred_element_type=jnp.float32
    )
    pert = jnp.einsum(
        "zlh,zhj->zlj",
        lower_bound,
        output_noise_factor.astype(jnp.float32),
        precision=lax.Precision.HIGHEST,
    )
    member_out = (base.reshape(members, tokens, -1) + 0.5 * pert).astype(jnp.bfloat16)
    pop_count = lax.axis_size("pop")
    total_members = ranks.shape[0] * pop_count
    fit = ranks.astype(jnp.float32) / (total_members - 1) - 0.5
    scaled_update = (output_noise_factor.astype(jnp.float32) * fit[:, None, None]).astype(
        jnp.bfloat16
    )
    weight_change = lax.psum_scatter(
        jnp.einsum(
            "vjs,vjg->sg", input_noise_factor, scaled_update, preferred_element_type=jnp.float32
        ),
        "pop",
        scatter_dimension=0,
        tiled=True,
    )
    mean_sq = lax.psum(jnp.sum(weight_change * weight_change), ("pop", "col")) / (D * F)
    step_dir = weight_change * lax.rsqrt(mean_sq + 1e-06)
    new_weight = (weight.astype(jnp.float32) + 0.01 * step_dir).astype(jnp.bfloat16)
    return (member_out, step_dir, new_weight)


def solution(mesh):
    in_specs = (
        P("pop", None, "col"),
        P("pop", "col"),
        P("pop", None, None),
        P("pop", None, "col"),
        P("pop"),
    )
    out_specs = (P("pop", None, "col"), P("pop", "col"), P("pop", "col"))
    return jax.shard_map(body, mesh=mesh, in_specs=in_specs, out_specs=out_specs, check_vma=False)
```

profile of v0, /device:TPU:1, one launch (start us, length us, event | category | flops | bytes accessed | tf_op | source)
XLA Modules:
  0.0 489.5 jit_solution(12580459237026647606)
XLA Ops:
  7.2 0.0 copy-start
  7.2 0.0 all-gather.3.cloned.1.call-start
  7.2 2.7 copy.13
  10.0 0.0 all-gather.3.cloned.1.call-update
  10.0 0.0 all-gather.5.cloned.1.call-start
  10.0 0.7 all-gather.5.cloned.1.call-update
  10.7 0.0 reduce-scatter.4.cloned.1.call-start
  10.8 0.7 multiply_add_fusion
  11.4 1.0 multiply_convert_fusion
  12.5 0.0 copy-done
  12.5 8.2 %convolution_bitcast_fusion = f32[3584,1184]{0,1:T(8,128)} fusion(bf16[16,4,3584]{2,1,0:T(4,128)(2,1)S(1)} %copy-done, bf16[16,4,1184]{2,1,0:T(4,128)(2,1)S(1)} %multiply_convert_fusion), kind=kOutput, calls=%fused_computation | convolution fusion | flops 543162368 | bytes 17584128 | tf_op jit(solution)/shard_map/vjs,vjg->sg/dot_general | solution.py:34
  20.7 19.0 %copy.20 = f32[3584,1184]{1,0:T(8,128)} copy(f32[3584,1184]{0,1:T(8,128)} %convolution_bitcast_fusion) | data formatting | bytes 33947648
  39.7 0.0 copy-start.3
  39.7 0.0 reduce-scatter.4.cloned.1.call-update
  39.7 1.2 copy-done.3
  41.0 1.5 copy.17
  42.5 71.7 %all-gather.3.cloned.1.call-done = bf16[16,64,3584]{1,0,2:T(8,128)(2,1)} async-done(((bf16[16,64,224]{1,0,2:T(8,128)(2,1)}), bf16[16,64,3584]{1,0,2:T(8,128)(2,1)}) %all-gather.3.cloned.1.call-update) | async-done | bytes 7340048 | tf_op jit(solution)/shard_map/all_gather | solution.py:11
  114.2 16.3 %copy.14 = bf16[16,64,3584]{2,1,0:T(8,128)(2,1)} copy(bf16[16,64,3584]{1,0,2:T(8,128)(2,1)} %all-gather.3.cloned.1.call-done) | data formatting | bytes 14680064 | tf_op jit(solution)/shard_map/all_gather | solution.py:11
  130.4 5.1 %fusion.4 = f32[16,64,4]{1,2,0:T(4,128)S(1)} fusion(bf16[16,64,3584]{2,1,0:T(8,128)(2,1)} %copy.14, bf16[16,4,3584]{2,1,0:T(4,128)(2,1)S(1)} %copy-done), kind=kOutput, calls=%fused_computation.11 | convolution fusion | flops 29360128 | bytes 7815168 | tf_op jit(solution)/shard_map/mtd,mrd->mtr/dot_general | solution.py:17
  135.5 76.5 %all-gather.5.cloned.1.call-done = bf16[3584,1184]{1,0:T(8,128)(2,1)} async-done(((bf16[448,1184]{1,0:T(8,128)(2,1)}), bf16[3584,1184]{1,0:T(8,128)(2,1)}) %all-gather.5.cloned.1.call-update) | async-done | bytes 8486928 | tf_op jit(solution)/shard_map/all_gather | solution.py:15
  212.0 16.1 %fusion = f32[16,64,1184]{2,1,0:T(8,128)} fusion(bf16[16,64,3584]{2,1,0:T(8,128)(2,1)} %copy.14, bf16[3584,1184]{1,0:T(8,128)(2,1)} %all-gather.5.cloned.1.call-done), kind=kOutput, calls=%fused_computation.1 | convolution fusion | flops 8690597888 | bytes 20676608 | tf_op jit(solution)/shard_map/dot_general | solution.py:14
  228.1 0.0 copy-start.4
  228.1 171.4 %reduce-scatter.4.cloned.1.call-done = f32[448,1184]{1,0:T(8,128)} async-done(((f32[3584,1184]{1,0:T(8,128)}), f32[448,1184]{1,0:T(8,128)}) %reduce-scatter.4.cloned.1.call-update) | async-done | bytes 2121744
  399.5 2.3 copy.21
  401.8 1.2 multiply_reduce_fusion
  403.0 0.0 copy-done.4
  403.1 6.3 %add_convert_fusion = bf16[16,64,1184]{2,1,0:T(8,128)(2,1)} fusion(f32[16,64,1184]{2,1,0:T(8,128)} %fusion, f32[16,64,4]{1,2,0:T(4,128)S(1)} %fusion.4, bf16[16,4,1184]{2,1,0:T(4,128)(2,1)S(1)} %copy-done.4), kind=kOutput, calls=%fused_computation.3 | convolution fusion | flops 61833216 | bytes 7442432 | tf_op jit(solution)/shard_map/zlh,zhj->zlj/dot_general | solution.py:20
  409.4 64.5 %psum.7 = f32[]{:T(128)} all-reduce(f32[]{:T(128)} %multiply_reduce_fusion), channel_id=1, replica_groups=mesh['pop'=8,'col'=16] {'pop','col'}, use_global_device_ids=true, to_apply=%region_2.0 | all-reduce | flops 1 | bytes 8 | tf_op jit(solution)/shard_map/psum | solution.py:41
  474.6 0.0 copy-start.1
  474.6 3.6 add_convert_fusion.1
  478.2 0.0 copy-start.2
  478.2 3.2 copy.18
  481.4 0.0 copy-done.2
  481.4 1.5 copy.19
  483.0 0.0 copy-done.1
Async XLA Ops:
  7.2 5.3 %copy-start = (bf16[16,4,3584]{2,1,0:T(4,128)(2,1)S(1)}, bf16[16,4,3584]{2,1,0:T(4,128)(2,1)}, u32[]{:S(2)}) copy-start(bf16[16,4,3584]{2,1,0:T(4,128)(2,1)} %param.7) | copy-start | bytes 1376260
  7.2 107.0 %all-gather.3.cloned.1.call-start = ((), (), s32[]{:S(2)}) async-start(), calls=%async_computation.1 | async-start | bytes 15597568 | tf_op jit(solution)/shard_map/all_gather | solution.py:11
  10.0 202.0 %all-gather.5.cloned.1.call-start = ((), (), s32[]{:S(2)}) async-start(), calls=%async_computation.2 | async-start | bytes 10321920 | tf_op jit(solution)/shard_map/all_gather | solution.py:15
  10.7 388.8 %reduce-scatter.4.cloned.1.call-start = ((), (), s32[]{:S(2)}) async-start(), calls=%async_computation.3 | async-start | bytes 20643840
  39.7 1.3 copy-start.3
  228.1 175.0 %copy-start.4 = (bf16[16,4,1184]{2,1,0:T(4,128)(2,1)S(1)}, bf16[16,4,1184]{2,1,0:T(4,128)(2,1)}, u32[]{:S(2)}) copy-start(bf16[16,4,1184]{2,1,0:T(4,128)(2,1)} %param.8) | copy-start | bytes 454660
  474.6 8.4 %copy-start.1 = (bf16[16,4,3584]{2,1,0:T(4,128)(2,1)S(1)}, bf16[16,4,3584]{2,1,0:T(4,128)(2,1)}, u32[]{:S(2)}) copy-start(bf16[16,4,3584]{2,1,0:T(4,128)(2,1)} %param.7) | copy-start | bytes 1376260
  478.2 3.2 copy-start.2
Sparse Core Ops, SparseCore 0:
  11.0 103.0 all-gather.2
  115.8 96.1 all-gather.4
  214.5 184.9 reduce-scatter.3
where the time goes:
time: 491 us; the launch traced here: 489 us
  waiting for transfers between devices  320 us (65%)
  blocking collectives  64.5 us (13%)
  local copies, waits for them, and re-layouts  47.8 us (10%)
  matrix products  35.7 us (7%)
  between operations  14.5 us (3%)
  other arithmetic  6.53 us (1%)
    unnamed x4, waiting for transfers between devices  172 us
    all_gather x1, waiting for transfers between devices, body(): lax.all_gather(weight, 'pop', axis=0, tiled=True)  76.5 us
    all_gather x1, waiting for transfers between devices, body(): whole = lax.all_gather(acts, 'col', axis=2, tiled=True)  71.7 us
    psum x1, blocking collectives, body(): lax.psum(jnp.sum(weight_change * weight_change), ('pop', 'col')) / (D * F)  64.5 us
    unnamed x16, local copies, waits for them, and re-layouts  31.5 us
    all_gather x1, local copies, waits for them, and re-layouts, body(): whole = lax.all_gather(acts, 'col', axis=2, tiled=True)  16.3 us
    dot_general x1, matrix products, body(): jnp.dot(flat, lax.all_gather(weight, 'pop', axis=0, tiled=True), preferre...  16.1 us
  transfers between devices with their start and end apart: 3, of which 3 were waited for; matrix products, arithmetic and copies ran while one was open for 14% of the time, Pallas kernels for 0%

commit v1 on v0

--- a/solution.py
+++ b/solution.py
@@ -7,8 +7,14 @@
 F = 18944
 
 
+def assign_the_quarters(x_local):
+    return jnp.concatenate(
+        lax.all_to_all(jnp.stack([x_local for _ in range(lax.axis_size("col"))]), "col", 0, 0), 2
+    )
+
+
 def body(acts, weight, input_noise_factor, output_noise_factor, ranks):
-    whole = lax.all_gather(acts, "col", axis=2, tiled=True)
+    whole = assign_the_quarters(acts)
     members, tokens, width = whole.shape
     flat = whole.reshape(members * tokens, width)
     base = jnp.dot(

time: 491 us -> 518 us (1.055)
  local copies, waits for them, and re-layouts: 47.8 us -> 61.9 us
  starting transfers between devices: 0.12 us -> 9.68 us
    all_to_all x0 -> x1, waiting for transfers between devices: none -> 324 us  [assign_the_quarters(): lax.all_to_all(jnp.stack([x_local for _ in range(lax.axis_size('col'))]),...]
    unnamed x4 -> x3, waiting for transfers between devices: 172 us -> 0.7 us
    all_gather x1, waiting for transfers between devices: 76.5 us -> 0.01 us  [body(): lax.all_gather(weight, 'pop', axis=0, tiled=True)]
    all_gather x1 -> x0, waiting for transfers between devices: 71.7 us -> none  [body(): whole = lax.all_gather(acts, 'col', axis=2, tiled=True)]
    dot_general x0 -> x1, local copies, waits for them, and re-layouts: none -> 16.6 us  [body(): jnp.dot(flat, lax.all_gather(weight, 'pop', axis=0, tiled=True), preferre...]
    all_gather x1 -> x0, local copies, waits for them, and re-layouts: 16.3 us -> none  [body(): whole = lax.all_gather(acts, 'col', axis=2, tiled=True)]
    reshape x0 -> x1, local copies, waits for them, and re-layouts: none -> 12.4 us  [assign_the_quarters(): jnp.concatenate(lax.all_to_all(jnp.stack([x_local for _ in range(lax.axis...]
    all_to_all x0 -> x1, starting transfers between devices: none -> 9.61 us  [assign_the_quarters(): lax.all_to_all(jnp.stack([x_local for _ in range(lax.axis_size('col'))]),...]
  transfers between devices with their start and end apart: 3 -> 3, of which waited for: 3 -> 1; matrix products, arithmetic and copies ran while one was open for 14% -> 16% of each run, Pallas kernels for 0% -> 0%
where the time goes in v1:
time: 518 us; the launch traced here: 516 us
  waiting for transfers between devices  325 us (63%)
  blocking collectives  62.8 us (12%)
  local copies, waits for them, and re-layouts  61.9 us (12%)
  matrix products  35.6 us (7%)
  between operations  14.8 us (3%)
  starting transfers between devices  9.68 us (2%)
  other arithmetic  6.48 us (1%)
    all_to_all x1, waiting for transfers between devices, assign_the_quarters(): lax.all_to_all(jnp.stack([x_local for _ in range(lax.axis_size('col'))]),...  324 us
    psum x1, blocking collectives, body(): lax.psum(jnp.sum(weight_change * weight_change), ('pop', 'col')) / (D * F)  62.8 us
    unnamed x15, local copies, waits for them, and re-layouts  28.5 us
    dot_general x1, local copies, waits for them, and re-layouts, body(): jnp.dot(flat, lax.all_gather(weight, 'pop', axis=0, tiled=True), preferre...  16.6 us
    dot_general x1, matrix products, body(): jnp.dot(flat, lax.all_gather(weight, 'pop', axis=0, tiled=True), preferre...  16.1 us
    reshape x1, local copies, waits for them, and re-layouts, assign_the_quarters(): jnp.concatenate(lax.all_to_all(jnp.stack([x_local for _ in range(lax.axis...  12.4 us
  transfers between devices with their start and end apart: 3, of which 1 were waited for; matrix products, arithmetic and copies ran while one was open for 16% of the time, Pallas kernels for 0%

profile of v1, /device:TPU:1, one launch (start us, length us, event | category | flops | bytes accessed | tf_op | source)
XLA Modules:
  0.0 516.3 jit_solution(10278297098495772513)
XLA Ops:
  7.2 0.0 copy-start
  7.2 0.0 all-gather.2.cloned.1.call-start
  7.2 0.7 all-gather.2.cloned.1.call-update
  7.9 0.0 reduce-scatter.4.cloned.1.call-start
  8.0 0.7 multiply_add_fusion
  8.6 1.0 multiply_convert_fusion
  9.7 0.0 copy-done
  9.7 8.2 %convolution_bitcast_fusion = f32[3584,1184]{0,1:T(8,128)} fusion(bf16[16,4,3584]{2,1,0:T(4,128)(2,1)S(1)} %copy-done, bf16[16,4,1184]{2,1,0:T(4,128)(2,1)S(1)} %multiply_convert_fusion), kind=kOutput, calls=%fused_computation | convolution fusion | flops 543162368 | bytes 17584128 | tf_op jit(solution)/shard_map/vjs,vjg->sg/dot_general | solution.py:40
  17.9 18.9 %copy.19 = f32[3584,1184]{1,0:T(8,128)} copy(f32[3584,1184]{0,1:T(8,128)} %convolution_bitcast_fusion) | data formatting | bytes 33947648
  36.7 0.0 copy-start.4
  36.7 0.0 reduce-scatter.4.cloned.1.call-update
  36.8 1.0 copy-done.4
  37.8 4.4 stack.2
  42.1 0.0 copy-start.2
  42.1 9.6 %all-to-all-start = ((bf16[16,16,64,224]{3,2,1,0:T(8,128)(2,1)}), bf16[16,16,64,224]{3,2,1,0:T(8,128)(2,1)}, u32[]{:S(2)}, u32[]{:S(2)}) async-start(bf16[16,16,64,224]{3,2,1,0:T(8,128)(2,1)} %stack.2), calls=%async_computation | async-start | bytes 16777216 | tf_op jit(solution)/shard_map/all_to_all | solution.py:12
  51.7 0.0 copy-done.2
  51.8 1.5 copy.16
  53.3 324.4 %all-to-all-done = bf16[16,16,64,224]{3,2,1,0:T(8,128)(2,1)} async-done(((bf16[16,16,64,224]{3,2,1,0:T(8,128)(2,1)}), bf16[16,16,64,224]{3,2,1,0:T(8,128)(2,1)}, u32[]{:S(2)}, u32[]{:S(2)}) %all-to-all-start) | async-done | bytes 7340064 | tf_op jit(solution)/shard_map/all_to_all | solution.py:12
  377.6 12.4 %copy.13 = bf16[16,64,16,224]{3,2,1,0:T(8,128)(2,1)} copy(bf16[16,64,16,224]{3,1,0,2:T(8,128)(2,1)} %bitcast) | data formatting | bytes 14680064 | tf_op jit(solution)/shard_map/reshape | solution.py:11
  390.0 16.6 %dot_general.16 = bf16[16,64,3584]{2,1,0:T(8,128)(2,1)} reshape(bf16[16,64,16,224]{3,2,1,0:T(8,128)(2,1)} %copy.13) | data formatting | bytes 14680064 | tf_op jit(solution)/shard_map/dot_general | solution.py:20
  406.6 5.1 fusion.4
  411.7 0.0 all-gather.2.cloned.1.call-done
  411.7 16.1 %fusion = f32[16,64,1184]{2,1,0:T(8,128)} fusion(bf16[16,64,3584]{2,1,0:T(8,128)(2,1)} %dot_general.16, bf16[3584,1184]{1,0:T(8,128)(2,1)} %all-gather.2.cloned.1.call-done), kind=kOutput, calls=%fused_computation.1 | convolution fusion | flops 8690597888 | bytes 20676608 | tf_op jit(solution)/shard_map/dot_general | solution.py:20
  427.8 0.0 copy-start.3
  427.8 0.0 reduce-scatter.4.cloned.1.call-done
  427.8 2.3 copy.20
  430.1 1.2 multiply_reduce_fusion
  431.3 0.0 copy-done.3
  431.3 6.3 %add_convert_fusion = bf16[16,64,1184]{2,1,0:T(8,128)(2,1)} fusion(f32[16,64,1184]{2,1,0:T(8,128)} %fusion, f32[16,64,4]{1,2,0:T(4,128)S(1)} %fusion.4, bf16[16,4,1184]{2,1,0:T(4,128)(2,1)S(1)} %copy-done.3), kind=kOutput, calls=%fused_computation.3 | convolution fusion | flops 61833216 | bytes 7442432 | tf_op jit(solution)/shard_map/zlh,zhj->zlj/dot_general | solution.py:26
  437.6 62.8 %psum.7 = f32[]{:T(128)} all-reduce(f32[]{:T(128)} %multiply_reduce_fusion), channel_id=1, replica_groups=mesh['pop'=8,'col'=16] {'pop','col'}, use_global_device_ids=true, to_apply=%region_2.0 | all-reduce | flops 1 | bytes 8 | tf_op jit(solution)/shard_map/psum | solution.py:47
  501.1 3.6 add_convert_fusion.1
  504.7 0.0 copy-start.1
  504.7 3.2 copy.17
  507.9 0.0 copy-done.1
  507.9 1.5 copy.18
Async XLA Ops:
  7.2 2.5 copy-start
  7.2 404.5 %all-gather.2.cloned.1.call-start = ((), (), s32[]{:S(2)}) async-start(), calls=%async_computation.2 | async-start | bytes 10321920 | tf_op jit(solution)/shard_map/all_gather | solution.py:21
  7.9 419.9 %reduce-scatter.4.cloned.1.call-start = ((), (), s32[]{:S(2)}) async-start(), calls=%async_computation.3 | async-start | bytes 20643840
  36.7 1.0 copy-start.4
  42.1 9.6 %copy-start.2 = (bf16[448,1184]{1,0:T(8,128)(2,1)S(1)}, bf16[448,1184]{1,0:T(8,128)(2,1)}, u32[]{:S(2)}) copy-start(bf16[448,1184]{1,0:T(8,128)(2,1)} %param.6) | copy-start | bytes 3182596
  42.1 335.5 %all-to-all-start = ((bf16[16,16,64,224]{3,2,1,0:T(8,128)(2,1)}), bf16[16,16,64,224]{3,2,1,0:T(8,128)(2,1)}, u32[]{:S(2)}, u32[]{:S(2)}) async-start(bf16[16,16,64,224]{3,2,1,0:T(8,128)(2,1)} %stack.2), calls=%async_computation | async-start | bytes 16777216 | tf_op jit(solution)/shard_map/all_to_all | solution.py:12
  427.8 3.6 copy-start.3
  504.7 3.2 copy-start.1
Sparse Core Ops, SparseCore 0:
  9.6 102.2 all-gather.1
  114.4 184.9 reduce-scatter.3
